TPU v7x, 32 devices: a whole 2x2x4 slice. The times are simulated.
32 devices in a mesh: half: 2 (over x), seq: 4 (over z), head: 4 (over y, core).
Axes of the slice: x: 2, y: 2, z: 4, core: 2. Of those that a mesh axis runs over, the one named last changes fastest.
Arguments:
- enc_states: bfloat16 [8192, 4096], P(('half', 'seq')), may hold values from -64 to 64
- norm_gain: float32 [4096], replicated, may hold values from 0.25 to 4
- kv_weight: bfloat16 [4096, 1024], P(None, 'head'), may hold values from -1 to 1
- queries: bfloat16 [1024, 4096], P(('half', 'seq'), 'head'), may hold values from -512 to 512
- cotangent: bfloat16 [1024, 4096], P(('half', 'seq'), 'head'), may hold values from -8 to 8
Outputs:
- context: bfloat16 [1024, 4096], P(('half', 'seq'), 'head')
- d_queries: bfloat16 [1024, 4096], P(('half', 'seq'), 'head')
- d_keys_values: bfloat16 [8192, 1024], P(('half', 'seq'), 'head')
All inputs are finite; a program needn't handle non-finite values.
Results may differ from a plain program's by a relative error of at most 0.013.
The roundings to bfloat16 on the way count: a program that leaves them out, or rounds other values in their place, can miss the bound.
Values may be sent and summed in bfloat16 or wider, within the bound.
No kernel may reach another device: no remote copies, remote signals or barrier semaphores. Data moves between devices by JAX's collectives and lax.ppermute only.
A program may use at most 128 MiB of HBM per device.

v0:
```python
import jax
import jax.numpy as jnp
from jax import lax
from jax.sharding import PartitionSpec as P

HD = 64
eps = 1e-06
block_rows = 1024


def block_of():
    return block_rows


def split_blocks(tensor):
    block_size = block_of()
    return tensor.reshape((tensor.shape[0] // block_size, block_size) + tensor.shape[1:])


def join_blocks(tensor):
    return tensor.reshape((tensor.shape[0] * tensor.shape[1],) + tensor.shape[2:])


def to_rows(matrix, groups, head_size):
    tokens = matrix.shape[0]
    per_group = matrix.shape[1] // (groups * head_size)
    shaped = matrix.reshape(tokens, groups, per_group, head_size).transpose(0, 2, 1, 3)
    return shaped.reshape(tokens * per_group, groups, head_size)


def from_rows(row_tensor, tokens):
    length, groups, head_size = row_tensor.shape
    per_group = length // tokens
    shaped = row_tensor.reshape(tokens, per_group, groups, head_size).transpose(0, 2, 1, 3)
    return shaped.reshape(tokens, groups * per_group * head_size)


def block_scores(query_block, pair_block, head_size):
    length = pair_block.shape[0]
    pieces = pair_block.reshape(length, -1, 2, head_size)
    key_rows = pieces[:, :, 0, :]
    values = pieces[:, :, 1, :]
    scores = jnp.einsum("rgd,bgd->rgb", query_block, key_rows, preferred_element_type=jnp.float32)
    return (scores * head_size ** (-0.5), key_rows, values)


def row_maxima(query_rows, pair_rows, head_size):

    def row_by_rows(query_block):

        def row_advance(largest, pair_block):
            scores = block_scores(query_block, pair_block, head_size)[0]
            return (jnp.maximum(largest, jnp.max(scores, axis=2)), None)

        initial = jnp.full(query_block.shape[:2], -jnp.inf, jnp.float32)
        return lax.scan(row_advance, initial, split_blocks(pair_rows))[0]

    return join_blocks(lax.map(row_by_rows, split_blocks(query_rows)))


def weighted_sums(query_rows, pair_rows, row_max, head_size):

    def weighted_by_rows(blocks):
        query_block, max_block = blocks

        def weighted_advance(running, pair_block):
            totals, accumulated = running
            scores, key_rows, values = block_scores(query_block, pair_block, head_size)
            exponent = jnp.exp(scores - max_block[:, :, None])
            accumulated = accumulated + jnp.einsum(
                "rgb,bgd->rgd",
                exponent.astype(jnp.bfloat16),
                values,
                preferred_element_type=jnp.float32,
            )
            return ((totals + jnp.sum(exponent, axis=2), accumulated), None)

        initial = (
            jnp.zeros(max_block.shape, jnp.float32),
            jnp.zeros(query_block.shape, jnp.float32),
        )
        return lax.scan(weighted_advance, initial, split_blocks(pair_rows))[0]

    totals, accumulated = lax.map(
        weighted_by_rows, (split_blocks(query_rows), split_blocks(row_max))
    )
    return (join_blocks(totals), join_blocks(accumulated))


def gradients(query_rows, grad_rows, pair_rows, row_max, totals, deltas, head_size):
    pair_blocks = split_blocks(pair_rows)

    def gradients_by_rows(pair_sum, blocks):
        query_block, grad_block, max_block, total_block, delta_block = blocks

        def gradients_advance(query_sum, pair_block):
            scores, key_rows, values = block_scores(query_block, pair_block, head_size)
            probability = jnp.exp(scores - max_block[:, :, None]) / total_block[:, :, None]
            prob_grad = jnp.einsum(
                "rgd,bgd->rgb", grad_block, values, preferred_element_type=jnp.float32
            )
            score_grad = (
                head_size ** (-0.5) * probability * (prob_grad - delta_block[:, :, None])
            ).astype(jnp.bfloat16)
            query_sum = query_sum + jnp.einsum(
                "rgb,bgd->rgd", score_grad, key_rows, preferred_element_type=jnp.float32
            )
            key_grad = jnp.einsum(
                "rgb,rgd->bgd", score_grad, query_block, preferred_element_type=jnp.float32
            )
            value_grad = jnp.einsum(
                "rgb,rgd->bgd",
                probability.astype(jnp.bfloat16),
                grad_block,
                preferred_element_type=jnp.float32,
            )
            return (
                query_sum,
                jnp.stack([key_grad, value_grad], axis=2).reshape(pair_block.shape[0], -1),
            )

        query_grad, pair_parts = lax.scan(
            gradients_advance, jnp.zeros(query_block.shape, jnp.float32), pair_blocks
        )
        return (pair_sum + pair_parts, query_grad)

    initial = jnp.zeros(pair_blocks.shape, jnp.float32)
    blocks = (
        split_blocks(query_rows),
        split_blocks(grad_rows),
        split_blocks(row_max),
        split_blocks(totals),
        split_blocks(deltas),
    )
    pair_grad, query_grad = lax.scan(gradients_by_rows, initial, blocks)
    return (join_blocks(query_grad), join_blocks(pair_grad))


def on_device(enc_states, norm_gain, kv_weight, queries, cotangent):
    groups = kv_weight.shape[1] // (2 * HD)
    states = enc_states.astype(jnp.float32)
    inverse_root = lax.rsqrt(jnp.mean(states * states, axis=1, keepdims=True) + eps)
    normed = (states * inverse_root * norm_gain).astype(jnp.bfloat16)
    own_pairs = jnp.dot(normed, kv_weight, preferred_element_type=jnp.float32).astype(jnp.bfloat16)
    tokens = queries.shape[0]
    query_rows = to_rows(queries, groups, HD)
    grad_rows = to_rows(cotangent, groups, HD)
    fragment = lax.all_gather(own_pairs, ("half", "seq"), axis=0, tiled=True)
    row_max = row_maxima(query_rows, fragment, HD)
    totals, accumulated = weighted_sums(query_rows, fragment, row_max, HD)
    context_rows = (accumulated / totals[:, :, None]).astype(jnp.bfloat16)
    deltas = jnp.sum(grad_rows.astype(jnp.float32) * context_rows.astype(jnp.float32), axis=2)
    query_grad, pair_grad = gradients(query_rows, grad_rows, fragment, row_max, totals, deltas, HD)
    pair_share = lax.psum_scatter(pair_grad, ("half", "seq"), scatter_dimension=0, tiled=True)
    context = from_rows(context_rows, tokens)
    d_queries = from_rows(query_grad.astype(jnp.bfloat16), tokens)
    return (context, d_queries, pair_share.astype(jnp.bfloat16))


def solution(mesh):
    placed = (
        P(("half", "seq"), None),
        P(),
        P(None, "head"),
        P(("half", "seq"), "head"),
        P(("half", "seq"), "head"),
    )
    return jax.shard_map(
        on_device,
        mesh=mesh,
        in_specs=placed,
        out_specs=(
            P(("half", "seq"), "head"),
            P(("half", "seq"), "head"),
            P(("half", "seq"), "head"),
        ),
        check_vma=False,
    )
```

profile of v0, /device:TPU:0, one launch (start us, length us, event | category | flops | bytes accessed | tf_op | source)
XLA Modules:
  0.0 438.9 jit_solution(8884652493314864029)
XLA Ops:
  7.2 5.2 %fusion.23 = f32[1024]{0:T(1024)S(1)} fusion(bf16[1024,4096]{1,0:T(8,128)(2,1)} %param.11), kind=kLoop, calls=%fused_computation.36 | loop fusion | flops 12581888 | bytes 8392704 | tf_op jit(solution)/shard_map/reduce_sum | solution.py:142
  13.6 4.0 fusion.30
  22.6 70.7 %all-gather.2.cloned.1.call-done = bf16[8192,256]{1,0:T(8,128)(2,1)} async-done(((bf16[1024,256]{1,0:T(8,128)(2,1)}), bf16[8192,256]{1,0:T(8,128)(2,1)}) %all-gather.2.cloned.1.call-update) | async-done | bytes 4194320 | tf_op jit(solution)/shard_map/all_gather | solution.py:148
  93.3 6.5 %copy.31 = bf16[8,1024,256]{1,2,0:T(8,128)(2,1)} copy(bf16[8,1024,256]{2,1,0:T(8,128)(2,1)} %bitcast.177) | data formatting | bytes 8388608
  99.8 19.5 %while.62 = (s32[]{:T(128)}, f32[1024,2]{0,1:T(2,128)S(1)}, bf16[8,1024,256]{1,2,0:T(8,128)(2,1)}, bf16[1024,2,64]{0,2,1:T(8,128)(2,1)S(1)}, s32[]{:T(128)}, /*index=5*/s32[]{:T(128)}) while((s32[]{:T(128)}, f32[1024,2]{0,1:T(2,128)S(1)}, bf16[8,1024,256]{1,2,0:T(8,128)(2,1)}, bf16[1024,2,64]{0,2,1:T(8,128)(2,1)S(1)}, s32[]{:T(128)}, ...), condition=%wide.region_3.0_spmd.clone, body=%wide.region_1.3_spmd.clone.sunk | while | flops 272631808 | bytes 1605723 | solution.py:56
  119.3 36.3 %while.63 = (s32[]{:T(128)}, f32[1024,2]{0,1:T(2,128)S(1)}, f32[1024,2,64]{0,2,1:T(8,128)S(1)}, bf16[8,1024,256]{1,2,0:T(8,128)(2,1)}, bf16[1024,2,64]{0,2,1:T(8...) while((s32[]{:T(128)}, f32[1024,2]{0,1:T(2,128)S(1)}, ...), condition=%wide.region_6.7_spmd.clone, body=%wide.region_4.0_spmd.clone.sunk | while | flops 549718016 | bytes 19710060 | solution.py:82
  157.1 2.6 multiply_reduce_fusion.1
  159.8 124.0 %while.64 = (s32[]{:T(128)}, f32[1024,2,64]{0,2,1:T(8,128)}, f32[8,1024,256]{2,1,0:T(8,128)}, bf16[8,1024,256]{1,2,0:T(8,128)(2,1)}, bf16[1024,2,64]{0,2,1:T(8,1...) while((s32[]{:T(128)}, f32[1024,2,64]{0,2,1:T(8,128)}, ...), condition=%wide.region_9.10_spmd.clone, body=%wide.region_8.9_spmd.clone.sunk | while | flops 1359478784 | bytes 51142788 | solution.py:122
  162.8 2.3 fusion.75
  165.1 2.3 fusion.73
  177.4 2.3 fusion.75
  179.7 2.3 fusion.73
  182.0 2.7 fusion.74
  193.0 2.3 fusion.75
  195.4 2.3 fusion.73
  197.6 2.7 fusion.74
  208.6 2.3 fusion.75
  211.0 2.3 fusion.73
  213.3 2.7 fusion.74
  224.2 2.3 fusion.75
  226.6 2.3 fusion.73
  228.9 2.7 fusion.74
  239.8 2.3 fusion.75
  242.2 2.3 fusion.73
  244.5 2.7 fusion.74
  255.5 2.3 fusion.75
  257.8 2.3 fusion.73
  260.1 2.7 fusion.74
  271.1 2.3 fusion.75
  273.5 2.3 fusion.73
  275.7 2.7 fusion.74
  288.5 141.5 %reduce-scatter.2.cloned.1.call-done = f32[1024,256]{1,0:T(8,128)} async-done(((f32[8192,256]{1,0:T(8,128)}), f32[1024,256]{1,0:T(8,128)}) %reduce-scatter.2.cloned.1.call-update) | async-done | bytes 1048592 | tf_op jit(solution)/shard_map/reduce_scatter | solution.py:154
  (147 shorter events, 137.5 us)
Async XLA Ops:
  7.2 5.3 %copy-start = (bf16[4096,256]{1,0:T(8,128)(2,1)S(1)}, bf16[4096,256]{1,0:T(8,128)(2,1)}, u32[]{:S(2)}) copy-start(bf16[4096,256]{1,0:T(8,128)(2,1)} %param.13) | copy-start | bytes 6291460
  7.2 86.1 %all-gather.2.cloned.1.call-start = ((), (), s32[]{:S(2)}) async-start(), calls=%async_computation.1 | async-start | bytes 4718592 | tf_op jit(solution)/shard_map/all_gather | solution.py:148
  7.2 6.4 %copy-start.1 = (bf16[1024,4096]{1,0:T(8,128)(2,1)S(1)}, bf16[1024,4096]{1,0:T(8,128)(2,1)}, u32[]{:S(2)}) copy-start(bf16[1024,4096]{1,0:T(8,128)(2,1)} %param.11) | copy-start | bytes 25165828
  13.6 4.3 copy-start.3
  17.6 412.3 %reduce-scatter.2.cloned.1.call-start = ((), (), s32[]{:S(2)}) async-start(), calls=%async_computation.2 | async-start | bytes 9437184 | tf_op jit(solution)/shard_map/reduce_scatter | solution.py:154
  283.7 1.0 copy-start.2
Sparse Core Ops, SparseCore 0:
  17.8 75.4 all-gather.1
  283.9 146.0 reduce-scatter.1
where the time goes:
time: 442 us; the launch traced here: 439 us
  waiting for transfers between devices  212 us (48%)
  matrix products  126 us (29%)
  local copies, waits for them, and re-layouts  73.6 us (17%)
  between operations  14.2 us (3%)
  other arithmetic  12 us (3%)
    reduce_scatter x1, waiting for transfers between devices, on_device(): lax.psum_scatter(pair_grad, ('half', 'seq'), scatter_dimension=0, tiled=T...  141 us
    all_gather x1, waiting for transfers between devices, on_device(): fragment = lax.all_gather(own_pairs, ('half', 'seq'), axis=0, tiled=True)  70.7 us
    dot_general x24, matrix products, block_scores(): jnp.einsum('rgd,bgd->rgb', query_block, key_rows, preferred_element_type=...  40 us
    dynamic_slice x24, local copies, waits for them, and re-layouts, row_by_rows(): return lax.scan(row_advance, initial, split_blocks(pair_rows))[0]  25.9 us
    dynamic_update_slice x16, local copies, waits for them, and re-layouts, gradients_by_rows(): lax.scan(gradients_advance, jnp.zeros(query_block.shape, jnp.float32), pa...  21 us
    dot_general x8, matrix products, gradients_advance(): jnp.einsum('rgb,bgd->rgd', score_grad, key_rows, preferred_element_type=j...  20.5 us
    dot_general x8, matrix products, gradients_advance(): jnp.einsum('rgb,rgd->bgd', probability.astype(jnp.bfloat16), grad_block,...  18.8 us
    dot_general x8, matrix products, gradients_advance(): jnp.einsum('rgd,bgd->rgb', grad_block, values, preferred_element_type=jnp...  18.3 us
  transfers between devices with their start and end apart: 2, of which 2 were waited for; matrix products, arithmetic and copies ran while one was open for 2% of the time, Pallas kernels for 0%

commit v1 on v0

--- a/solution.py
+++ b/solution.py
@@ -145,7 +145,12 @@
     tokens = queries.shape[0]
     query_rows = to_rows(queries, groups, HD)
     grad_rows = to_rows(cotangent, groups, HD)
-    fragment = lax.all_gather(own_pairs, ("half", "seq"), axis=0, tiled=True)
+    fragment = jnp.concatenate(
+        lax.all_to_all(
+            jnp.stack([own_pairs] * lax.axis_size(("half", "seq"))), ("half", "seq"), 0, 0
+        ),
+        axis=0,
+    )
     row_max = row_maxima(query_rows, fragment, HD)
     totals, accumulated = weighted_sums(query_rows, fragment, row_max, HD)
     context_rows = (accumulated / totals[:, :, None]).astype(jnp.bfloat16)

time: 442 us -> 461 us (1.043)
  waiting for transfers between devices: 212 us -> 230 us
  starting transfers between devices: 0.26 us -> 7.31 us
    all_to_all x0 -> x1, waiting for transfers between devices: none -> 89.4 us  [on_device(): lax.all_to_all(jnp.stack([own_pairs] * lax.axis_size(('half', 'seq'))), (...]
    all_gather x1 -> x0, waiting for transfers between devices: 70.7 us -> none  [on_device(): fragment = lax.all_gather(own_pairs, ('half', 'seq'), axis=0, tiled=True)]
    all_to_all x0 -> x1, starting transfers between devices: none -> 7.28 us  [on_device(): lax.all_to_all(jnp.stack([own_pairs] * lax.axis_size(('half', 'seq'))), (...]
    unnamed x15 -> x18, local copies, waits for them, and re-layouts: 13.4 us -> 6.96 us
where the time goes in v1:
time: 461 us; the launch traced here: 459 us
  waiting for transfers between devices  230 us (50%)
  matrix products  125 us (27%)
  local copies, waits for them, and re-layouts  69.8 us (15%)
  between operations  14.2 us (3%)
  other arithmetic  12 us (3%)
  starting transfers between devices  7.31 us (2%)
    reduce_scatter x1, waiting for transfers between devices, on_device(): lax.psum_scatter(pair_grad, ('half', 'seq'), scatter_dimension=0, tiled=T...  140 us
    all_to_all x1, waiting for transfers between devices, on_device(): lax.all_to_all(jnp.stack([own_pairs] * lax.axis_size(('half', 'seq'))), (...  89.4 us
    dot_general x24, matrix products, block_scores(): jnp.einsum('rgd,bgd->rgb', query_block, key_rows, preferred_element_type=...  40 us
    dynamic_slice x24, local copies, waits for them, and re-layouts, row_by_rows(): return lax.scan(row_advance, initial, split_blocks(pair_rows))[0]  25.9 us
    dynamic_update_slice x16, local copies, waits for them, and re-layouts, gradients_by_rows(): lax.scan(gradients_advance, jnp.zeros(query_block.shape, jnp.float32), pa...  20.9 us
    dot_general x8, matrix products, gradients_advance(): jnp.einsum('rgb,bgd->rgd', score_grad, key_rows, preferred_element_type=j...  20.5 us
    dot_general x8, matrix products, gradients_advance(): jnp.einsum('rgb,rgd->bgd', probability.astype(jnp.bfloat16), grad_block,...  18.8 us
    dot_general x8, matrix products, gradients_advance(): jnp.einsum('rgd,bgd->rgb', grad_block, values, preferred_element_type=jnp...  18.3 us
  transfers between devices with their start and end apart: 2, of which 2 were waited for; matrix products, arithmetic and copies ran while one was open for 2% of the time, Pallas kernels for 0%

profile of v1, /device:TPU:0, one launch (start us, length us, event | category | flops | bytes accessed | tf_op | source)
XLA Modules:
  0.0 458.7 jit_solution(18422508179417039434)
XLA Ops:
  7.2 5.2 %fusion.23 = f32[1024]{0:T(1024)S(1)} fusion(bf16[1024,4096]{1,0:T(8,128)(2,1)} %param.11), kind=kLoop, calls=%fused_computation.36 | loop fusion | flops 12581888 | bytes 8392704 | tf_op jit(solution)/shard_map/reduce_sum | solution.py:142
  13.6 3.2 fusion.30
  17.0 2.5 stack.8
  19.5 7.3 %all-to-all-start = ((bf16[8,1024,256]{1,2,0:T(8,128)(2,1)}), bf16[8,1024,256]{1,2,0:T(8,128)(2,1)}, u32[]{:S(2)}, u32[]{:S(2)}) async-start(bf16[8,1024,256]{1,2,0:T(8,128)(2,1)} %stack.8), calls=%async_computation | async-start | bytes 8388608 | tf_op jit(solution)/shard_map/all_to_all | solution.py:149
  31.5 89.4 %all-to-all-done = bf16[8,1024,256]{1,2,0:T(8,128)(2,1)} async-done(((bf16[8,1024,256]{1,2,0:T(8,128)(2,1)}), bf16[8,1024,256]{1,2,0:T(8,128)(2,1)}, u32[]{:S(2)}, u32[]{:S(2)}) %all-to-all-start) | async-done | bytes 4194336 | tf_op jit(solution)/shard_map/all_to_all | solution.py:149
  120.9 19.5 %while.62 = (s32[]{:T(128)}, f32[1024,2]{0,1:T(2,128)S(1)}, bf16[8,1024,256]{1,2,0:T(8,128)(2,1)}, bf16[1024,2,64]{0,2,1:T(8,128)(2,1)S(1)}, s32[]{:T(128)}, /*index=5*/s32[]{:T(128)}) while((s32[]{:T(128)}, f32[1024,2]{0,1:T(2,128)S(1)}, bf16[8,1024,256]{1,2,0:T(8,128)(2,1)}, bf16[1024,2,64]{0,2,1:T(8,128)(2,1)S(1)}, s32[]{:T(128)}, ...), condition=%wide.region_3.0_spmd.clone, body=%wide.region_1.3_spmd.clone.sunk | while | flops 272631808 | bytes 1605723 | solution.py:56
  140.4 36.4 %while.63 = (s32[]{:T(128)}, f32[1024,2]{0,1:T(2,128)S(1)}, f32[1024,2,64]{0,2,1:T(8,128)S(1)}, bf16[8,1024,256]{1,2,0:T(8,128)(2,1)}, bf16[1024,2,64]{0,2,1:T(8...) while((s32[]{:T(128)}, f32[1024,2]{0,1:T(2,128)S(1)}, ...), condition=%wide.region_6.7_spmd.clone, body=%wide.region_4.0_spmd.clone.sunk | while | flops 549718016 | bytes 19710060 | solution.py:82
  178.3 2.6 multiply_reduce_fusion.1
  181.0 123.8 %while.64 = (s32[]{:T(128)}, f32[1024,2,64]{0,2,1:T(8,128)}, f32[8,1024,256]{2,1,0:T(8,128)}, bf16[8,1024,256]{1,2,0:T(8,128)(2,1)}, bf16[1024,2,64]{0,2,1:T(8,1...) while((s32[]{:T(128)}, f32[1024,2,64]{0,2,1:T(8,128)}, ...), condition=%wide.region_9.10_spmd.clone, body=%wide.region_8.9_spmd.clone.sunk | while | flops 1359478784 | bytes 51142788 | solution.py:122
  184.0 2.3 fusion.75
  186.3 2.3 fusion.73
  198.5 2.3 fusion.75
  200.9 2.3 fusion.73
  203.2 2.7 fusion.74
  214.2 2.3 fusion.75
  216.5 2.3 fusion.73
  218.8 2.7 fusion.74
  229.8 2.3 fusion.75
  234.4 2.7 fusion.74
  245.4 2.3 fusion.75
  247.7 2.3 fusion.73
  250.0 2.7 fusion.74
  260.9 2.3 fusion.75
  263.3 2.3 fusion.73
  265.6 2.7 fusion.74
  276.6 2.3 fusion.75
  278.9 2.3 fusion.73
  281.2 2.7 fusion.74
  292.2 2.3 fusion.75
  294.5 2.3 fusion.73
  296.8 2.7 fusion.74
  309.6 140.2 %reduce-scatter.2.cloned.1.call-done = f32[1024,256]{1,0:T(8,128)} async-done(((f32[8192,256]{1,0:T(8,128)}), f32[1024,256]{1,0:T(8,128)}) %reduce-scatter.2.cloned.1.call-update) | async-done | bytes 1048592 | tf_op jit(solution)/shard_map/reduce_scatter | solution.py:159
  (151 shorter events, 139.7 us)
Async XLA Ops:
  7.2 5.3 %copy-start = (bf16[4096,256]{1,0:T(8,128)(2,1)S(1)}, bf16[4096,256]{1,0:T(8,128)(2,1)}, u32[]{:S(2)}) copy-start(bf16[4096,256]{1,0:T(8,128)(2,1)} %param.13) | copy-start | bytes 6291460
  7.2 6.4 %copy-start.1 = (bf16[1024,4096]{1,0:T(8,128)(2,1)S(1)}, bf16[1024,4096]{1,0:T(8,128)(2,1)}, u32[]{:S(2)}) copy-start(bf16[1024,4096]{1,0:T(8,128)(2,1)} %param.11) | copy-start | bytes 25165828
  17.0 9.9 %copy-start.5 = (bf16[128,1024]{1,0:T(8,128)(2,1)S(1)}, bf16[128,1024]{1,0:T(8,128)(2,1)}, u32[]{:S(2)}) copy-start(bf16[128,1024]{1,0:T(8,128)(2,1)} %param.14) | copy-start | bytes 786436
  19.5 101.4 %all-to-all-start = ((bf16[8,1024,256]{1,2,0:T(8,128)(2,1)}), bf16[8,1024,256]{1,2,0:T(8,128)(2,1)}, u32[]{:S(2)}, u32[]{:S(2)}) async-start(bf16[8,1024,256]{1,2,0:T(8,128)(2,1)} %stack.8), calls=%async_computation | async-start | bytes 8388608 | tf_op jit(solution)/shard_map/all_to_all | solution.py:149
  26.8 423.0 %reduce-scatter.2.cloned.1.call-start = ((), (), s32[]{:S(2)}) async-start(), calls=%async_computation.2 | async-start | bytes 9437184 | tf_op jit(solution)/shard_map/reduce_scatter | solution.py:159
  30.6 90.3 %copy-start.2 = (bf16[128,2,8,64]{3,2,0,1:T(8,128)(2,1)}, bf16[128,2,8,64]{3,2,0,1:T(8,128)(2,1)S(1)}, u32[]{:S(2)}) copy-start(bf16[128,2,8,64]{3,2,0,1:T(8,128)(2,1)S(1)} %copy.35) | copy-start | bytes 786436
  140.4 37.9 %copy-start.3 = (bf16[128,2,8,64]{3,2,0,1:T(8,128)(2,1)S(1)}, bf16[128,2,8,64]{3,2,0,1:T(8,128)(2,1)}, u32[]{:S(2)}) copy-start(bf16[128,2,8,64]{3,2,0,1:T(8,128)(2,1)} %copy-done.2) | copy-start | bytes 786436
  304.8 1.0 copy-start.4
Sparse Core Ops, SparseCore 0:
  304.9 144.8 reduce-scatter.1
